TPU v7x, 512 devices: a whole 4x4x16 slice. The times are simulated.
512 devices in a mesh: row: 4 (over x), col: 128 (over y, z, core).
Axes of the slice: x: 4, y: 4, z: 16, core: 2. Of those that a mesh axis runs over, the one named last changes fastest.
Arguments:
- a_matrix: bfloat16 [4096, 65536], P('row', 'col'), may hold values from -0.0234375 to 0.0234375
- omega: bfloat16 [96, 65536], P(None, 'col'), may hold values from -6 to 6
- col_scale: float32 [65536], P('col'), may hold values from 1 to 48
- cone_point: float32 [4096], P('row'), may hold values from -8 to 8, as said below
- cone_id: int32 [4096], P('row'), may hold values from 0 to 4095, as said below
- cone_kind: int32 [4096], P('row'), may hold values from 0 to 1, as said below
Outputs:
- q_basis: float32 [96, 65536], P(None, 'col')
- r_factor: float32 [96, 96], replicated
Inputs may be any that keep to these rules, and one draw needn't show every extreme that they name: `cone_id`: rows of one cone are consecutive and share one id, the index of the cone's first row; every cone lies inside an aligned block of 4 rows; the last row is a cone of its own. `cone_kind`: 1 marks a second-order cone, 0 nonnegative entries; equal on all rows of a cone; 1 only on cones of two rows or more. `cone_point`: on a second-order cone every non-head entry has magnitude 0.5 or more, and the head's magnitude is at most 0.95 times the norm of the other entries.
All inputs are finite; a program needn't handle non-finite values.
Results may differ from a plain program's by a relative error of at most 0.014.
Values may be sent and summed in bfloat16 or wider, within the bound.
A program may use at most 64 MiB of HBM per device.

v0:
```python
import jax
import jax.numpy as jnp
from jax import lax
from jax.sharding import Mesh
from jax.sharding import PartitionSpec as P

CONE_SPAN = 4
PASSES = 2
COL = ("col_0", "col_1", "col_2")


def sum_in_order(parts, axes, order):
    inside = parts.shape[1:]
    parts = parts.reshape(*(lax.axis_size(a) for a in axes), *inside)
    parts = jnp.moveaxis(parts, order, range(len(axes))).reshape(-1, *inside)
    for k in order:
        parts = lax.psum_scatter(parts, axes[k], scatter_dimension=0, tiled=True)
    return parts[0]


def cut_along(shard, dim, devices):
    lengths = shard.shape
    parts = shard.reshape(*lengths[:dim], devices, lengths[dim] // devices, *lengths[dim + 1 :])
    return jnp.moveaxis(parts, dim, 0)


def summed_rows(shard, axes, order, dim):
    devices = lax.axis_size(axes)
    return sum_in_order(cut_along(shard, dim, devices), axes, order)


def joined_along(parts, dim):
    lengths = list(parts.shape[1:])
    lengths[dim] *= parts.shape[0]
    return jnp.moveaxis(parts, 0, dim).reshape(lengths)


def all_blocks(shard, axes, order):
    parts = shard
    for k in order:
        parts = lax.all_gather(parts, axes[k])
    done = order[::-1]
    back = [done.index(k) for k in range(len(axes))]
    parts = parts.transpose(*back, *range(len(axes), parts.ndim))
    return parts.reshape(-1, *shard.shape)


def gathered_by_axis(shard, axes, order, dim):
    return joined_along(all_blocks(shard, axes, order), dim)


def sent_to_all(shard, axis):
    devices = lax.axis_size(axis)
    return lax.all_to_all(
        jnp.broadcast_to(shard[None], (devices, *shard.shape)), axis, 0, 0, tiled=True
    )


def taken_together(shard, axis):
    return sent_to_all(shard, axis).astype(jnp.float32).sum(axis=0)


def by_axis(shard, axes):
    for axis in axes:
        shard = lax.psum(shard, axis)
    return shard


def cone_operator(cone_vals, cone_ids, cone_types):
    length = cone_vals.shape[0]
    span_len = CONE_SPAN
    blocks = length // span_len
    previous = jnp.concatenate([cone_ids[:1] - 1, cone_ids[:-1]])
    is_head = cone_ids != previous
    second_order = cone_types == 1
    tail_vals = jnp.where(second_order & ~is_head, cone_vals, jnp.float32(0.0))
    block_ids = cone_ids.reshape(blocks, span_len)
    same_cone = (block_ids[:, :, None] == block_ids[:, None, :]).astype(jnp.float32)
    tail_block = tail_vals.reshape(blocks, span_len)
    head_only = jnp.where(is_head, cone_vals, jnp.float32(0.0)).reshape(blocks, span_len)
    tail_sq = jnp.sum(same_cone * (tail_block * tail_block)[:, None, :], axis=2)
    head_vals = jnp.sum(same_cone * head_only[:, None, :], axis=2)
    soc_block = second_order.reshape(blocks, span_len)
    head_block = is_head.reshape(blocks, span_len)
    tail_norm = jnp.sqrt(jnp.where(soc_block, tail_sq, jnp.float32(1.0)))
    cone_ratio = head_vals / tail_norm
    unit_tail = tail_block / tail_norm
    identity_mat = jnp.eye(span_len, dtype=jnp.float32)
    head_rows = 0.5 * (identity_mat[None, :, :] + unit_tail[:, None, :])
    tail_rows = 0.5 * (
        unit_tail[:, :, None] * head_block[:, None, :].astype(jnp.float32)
        + (1.0 + cone_ratio)[:, :, None] * identity_mat[None, :, :]
        - cone_ratio[:, :, None] * unit_tail[:, :, None] * unit_tail[:, None, :]
    )
    soc_rows = jnp.where(head_block[:, :, None], head_rows, tail_rows)
    positive = jnp.where(cone_vals > 0, jnp.float32(1.0), jnp.float32(0.0)).reshape(
        blocks, span_len
    )
    plain_rows = identity_mat[None, :, :] * positive[:, :, None]
    return same_cone * jnp.where(soc_block[:, :, None], soc_rows, plain_rows)


def apply_cones(sketch_rows, operator):
    blocks = operator.shape[0]
    span_len = operator.shape[1]
    width = sketch_rows.shape[0]
    shaped = sketch_rows.reshape(width, blocks, span_len)
    result = jnp.zeros((width, blocks, span_len), jnp.float32)
    for inner in range(span_len):
        result = result + shaped[:, :, inner : inner + 1] * operator[None, :, :, inner]
    return result.reshape(width, blocks * span_len)


def local(a_matrix, omega, col_scale, cone_point, cone_id, cone_kind):
    row_count = a_matrix.shape[0]
    col_count = a_matrix.shape[1]
    total_cols = col_count * lax.axis_size(COL)
    share_rows = row_count // lax.axis_size(COL)
    first_row = lax.axis_index(COL) * share_rows
    operator = cone_operator(
        lax.dynamic_slice_in_dim(cone_point, first_row, share_rows),
        lax.dynamic_slice_in_dim(cone_id, first_row, share_rows),
        lax.dynamic_slice_in_dim(cone_kind, first_row, share_rows),
    )
    vectors = omega
    for repeat in range(PASSES):
        scaled = (vectors.astype(jnp.float32) * col_scale[None, :]).astype(jnp.bfloat16)
        partial_value = lax.dot_general(
            scaled, a_matrix, (((1,), (1,)), ((), ())), preferred_element_type=jnp.float32
        )
        owned = summed_rows(partial_value, COL, (2, 1, 0), 1)
        weighted = apply_cones(owned, operator).astype(jnp.bfloat16)
        back = jnp.dot(
            gathered_by_axis(weighted, COL, (0, 1, 2), 1),
            a_matrix,
            preferred_element_type=jnp.float32,
        )
        summed_back = (
            taken_together(back.astype(jnp.bfloat16), "row").astype(jnp.float32)
            * col_scale[None, :]
        )
        local_gram = jnp.dot(summed_back, summed_back.T, precision=lax.Precision.HIGHEST)
        gram_matrix = by_axis(local_gram, COL) / total_cols
        lower_factor = jnp.linalg.cholesky(gram_matrix)
        orth_basis = lax.linalg.triangular_solve(
            lower_factor, summed_back, left_side=True, lower=True
        )
        vectors = orth_basis.astype(jnp.bfloat16)
    return (orth_basis, lower_factor.T)


def solution(mesh):
    split = Mesh(
        mesh.devices.reshape(mesh.shape["row"], 4, 16, 2), ("row", "col_0", "col_1", "col_2")
    )
    in_specs = (P("row", COL), P(None, COL), P(COL), P("row"), P("row"), P("row"))
    out_specs = (P(None, COL), P())
    return jax.shard_map(local, mesh=split, in_specs=in_specs, out_specs=out_specs, check_vma=False)
```

profile of v0, /device:TPU:1, one launch (start us, length us, event | category | flops | bytes accessed | tf_op | source)
XLA Modules:
  0.0 530.2 jit_solution(10791986055114302990)
XLA Ops:
  14.1 21.8 %reduce-scatter.5.cloned.1.call-done = f32[64,96,8]{1,2,0:T(8,128)} async-done(((f32[128,96,8]{1,2,0:T(8,128)}), f32[64,96,8]{1,2,0:T(8,128)}) %reduce-scatter.5.cloned.1.call-update) | async-done | bytes 196624 | tf_op jit(solution)/shard_map/reduce_scatter | solution.py:17
  37.7 59.0 %reduce-scatter.7.cloned.1.call-done = f32[4,96,8]{1,2,0:T(8,128)} async-done(((f32[64,96,8]{1,2,0:T(8,128)}), f32[4,96,8]{1,2,0:T(8,128)}) %reduce-scatter.7.cloned.1.call-update) | async-done | bytes 12304 | tf_op jit(solution)/shard_map/reduce_scatter | solution.py:17
  96.7 14.1 %all-reduce = f32[4,96,8]{1,2,0:T(8,128)S(1)} all-reduce(f32[4,96,8]{1,2,0:T(8,128)} %reduce-scatter.7.cloned.1.call-done), channel_id=8, replica_groups=mesh['row'=4,'col_0'=4,'col_1'=16,'col_2'=2] {'col_0'}, use_global_device_ids=true, to_apply=%region_2.3.clone | all-reduce | flops 3072 | bytes 24576
  111.5 8.4 %all_gather.32 = bf16[4,96,8]{1,2,0:T(8,128)(2,1)S(1)} all-gather(bf16[1,96,8]{1,2,0:T(8,128)(2,1)S(1)} %add_convert_fusion.1), channel_id=1, replica_groups=mesh['row'=4,'col_0'=4,'col_1'=16,'col_2'=2] {'col_0'}, dimensions={0}, use_global_device_ids=true | all-gather | bytes 7680 | tf_op jit(solution)/shard_map/all_gather | solution.py:41
  120.0 20.8 %all-gather = bf16[64,96,8]{1,2,0:T(8,128)(2,1)S(1)} all-gather(bf16[4,96,8]{1,2,0:T(8,128)(2,1)S(1)} %all_gather.32), channel_id=2, replica_groups=mesh['row'=4,'col_0'=4,'col_1'=16,'col_2'=2] {'col_1'}, dimensions={0}, use_global_device_ids=true | all-gather | bytes 104448 | tf_op jit(solution)/shard_map/all_gather | solution.py:41
  140.8 26.4 %all-gather.1 = bf16[32,4,96,8]{2,3,1,0:T(8,128)(2,1)S(1)} all-gather(bf16[16,4,96,8]{2,3,1,0:T(8,128)(2,1)S(1)} %bitcast.98), channel_id=3, replica_groups=mesh['row'=4,'col_0'=4,'col_1'=16,'col_2'=2] {'col_2'}, dimensions={0}, use_global_device_ids=true | all-gather | bytes 294912 | tf_op jit(solution)/shard_map/all_gather | solution.py:41
  167.7 11.0 %all_to_all.10 = bf16[4,96,512]{2,1,0:T(8,128)(2,1)S(1)} all-to-all(bf16[4,96,512]{2,1,0:T(8,128)(2,1)S(1)} %broadcast_in_dim.66), channel_id=1, replica_groups=mesh['row'=4,'col_0'=4,'col_1'=16,'col_2'=2] {'row'}, dimensions={0} | all-to-all | bytes 786432 | tf_op jit(solution)/shard_map/all_to_all | solution.py:54
  179.7 11.2 %psum.42 = f32[96,96]{0,1:T(8,128)S(1)} all-reduce(f32[96,96]{0,1:T(8,128)S(1)} %fusion.8), channel_id=1, replica_groups=mesh['row'=4,'col_0'=4,'col_1'=16,'col_2'=2] {'col_0'}, use_global_device_ids=true, to_apply=%region_6.7 | all-reduce | flops 9216 | bytes 73728 | tf_op jit(solution)/shard_map/psum | solution.py:65
  190.9 40.5 %psum.43 = f32[96,96]{0,1:T(8,128)S(1)} all-reduce(f32[96,96]{0,1:T(8,128)S(1)} %psum.42), channel_id=1, replica_groups=mesh['row'=4,'col_0'=4,'col_1'=16,'col_2'=2] {'col_1'}, use_global_device_ids=true, to_apply=%region_7.8 | all-reduce | flops 9216 | bytes 73728 | tf_op jit(solution)/shard_map/psum | solution.py:65
  231.4 22.6 %psum.44 = f32[96,96]{0,1:T(8,128)S(1)} all-reduce(f32[96,96]{0,1:T(8,128)S(1)} %psum.43), channel_id=1, replica_groups=mesh['row'=4,'col_0'=4,'col_1'=16,'col_2'=2] {'col_2'}, use_global_device_ids=true, to_apply=%region_8.9 | all-reduce | flops 9216 | bytes 73728 | tf_op jit(solution)/shard_map/psum | solution.py:65
  254.1 8.8 %cholesky.44 = f32[96,96]{1,0:T(8,128)S(1)} custom-call(f32[96,96]{1,0:T(8,128)S(1)} %fusion.20), custom_call_target="Cholesky" | custom-call | tf_op jit(solution)/shard_map/jit(cholesky)/cholesky | solution.py:144
  264.3 7.4 %custom-call.6 = f32[1,96,96]{1,2,0:T(8,128)S(1)} custom-call(f32[1,96,96]{2,1,0:T(8,128)S(1)} %fusion.16), custom_call_target="InvertDiagBlocksLowerTriangular" | custom-call | tf_op jit(solution)/shard_map/triangular_solve/custom-call.0 | solution.py:145
  273.4 13.7 %reduce-scatter.9.cloned.1.call-done = f32[64,96,8]{1,2,0:T(8,128)} async-done(((f32[128,96,8]{1,2,0:T(8,128)}), f32[64,96,8]{1,2,0:T(8,128)}) %reduce-scatter.9.cloned.1.call-update) | async-done | bytes 196624 | tf_op jit(solution)/shard_map/reduce_scatter | solution.py:17
  287.1 60.6 %reduce-scatter.11.cloned.1.call-done = f32[4,96,8]{1,2,0:T(8,128)} async-done(((f32[64,96,8]{1,2,0:T(8,128)}), f32[4,96,8]{1,2,0:T(8,128)}) %reduce-scatter.11.cloned.1.call-update) | async-done | bytes 12304 | tf_op jit(solution)/shard_map/reduce_scatter | solution.py:17
  347.6 14.0 %all-reduce.1 = f32[4,96,8]{1,2,0:T(8,128)S(1)} all-reduce(f32[4,96,8]{1,2,0:T(8,128)} %reduce-scatter.11.cloned.1.call-done), channel_id=11, replica_groups=mesh['row'=4,'col_0'=4,'col_1'=16,'col_2'=2] {'col_0'}, use_global_device_ids=true, to_apply=%region_13.16.clone | all-reduce | flops 3072 | bytes 24576
  362.5 8.4 %all_gather.37 = bf16[4,96,8]{1,2,0:T(8,128)(2,1)S(1)} all-gather(bf16[1,96,8]{1,2,0:T(8,128)(2,1)S(1)} %add_convert_fusion), channel_id=1, replica_groups=mesh['row'=4,'col_0'=4,'col_1'=16,'col_2'=2] {'col_0'}, dimensions={0}, use_global_device_ids=true | all-gather | bytes 7680 | tf_op jit(solution)/shard_map/all_gather | solution.py:41
  370.9 20.9 %all-gather.2 = bf16[64,96,8]{1,2,0:T(8,128)(2,1)S(1)} all-gather(bf16[4,96,8]{1,2,0:T(8,128)(2,1)S(1)} %all_gather.37), channel_id=4, replica_groups=mesh['row'=4,'col_0'=4,'col_1'=16,'col_2'=2] {'col_1'}, dimensions={0}, use_global_device_ids=true | all-gather | bytes 104448 | tf_op jit(solution)/shard_map/all_gather | solution.py:41
  391.8 26.4 %all-gather.3 = bf16[32,4,96,8]{2,3,1,0:T(8,128)(2,1)S(1)} all-gather(bf16[16,4,96,8]{2,3,1,0:T(8,128)(2,1)S(1)} %bitcast.99), channel_id=5, replica_groups=mesh['row'=4,'col_0'=4,'col_1'=16,'col_2'=2] {'col_2'}, dimensions={0}, use_global_device_ids=true | all-gather | bytes 294912 | tf_op jit(solution)/shard_map/all_gather | solution.py:41
  418.7 10.8 %all_to_all.11 = bf16[4,96,512]{2,1,0:T(8,128)(2,1)S(1)} all-to-all(bf16[4,96,512]{2,1,0:T(8,128)(2,1)S(1)} %broadcast_in_dim.67), channel_id=1, replica_groups=mesh['row'=4,'col_0'=4,'col_1'=16,'col_2'=2] {'row'}, dimensions={0} | all-to-all | bytes 786432 | tf_op jit(solution)/shard_map/all_to_all | solution.py:54
  429.9 11.2 %psum.45 = f32[96,96]{0,1:T(8,128)S(1)} all-reduce(f32[96,96]{0,1:T(8,128)S(1)} %fusion.5), channel_id=1, replica_groups=mesh['row'=4,'col_0'=4,'col_1'=16,'col_2'=2] {'col_0'}, use_global_device_ids=true, to_apply=%region_15.18 | all-reduce | flops 9216 | bytes 73728 | tf_op jit(solution)/shard_map/psum | solution.py:65
  441.1 40.5 %psum.46 = f32[96,96]{0,1:T(8,128)S(1)} all-reduce(f32[96,96]{0,1:T(8,128)S(1)} %psum.45), channel_id=1, replica_groups=mesh['row'=4,'col_0'=4,'col_1'=16,'col_2'=2] {'col_1'}, use_global_device_ids=true, to_apply=%region_16.19 | all-reduce | flops 9216 | bytes 73728 | tf_op jit(solution)/shard_map/psum | solution.py:65
  481.5 22.8 %psum.47 = f32[96,96]{0,1:T(8,128)S(1)} all-reduce(f32[96,96]{0,1:T(8,128)S(1)} %psum.46), channel_id=1, replica_groups=mesh['row'=4,'col_0'=4,'col_1'=16,'col_2'=2] {'col_2'}, use_global_device_ids=true, to_apply=%region_17.20 | all-reduce | flops 9216 | bytes 73728 | tf_op jit(solution)/shard_map/psum | solution.py:65
  504.5 8.8 %cholesky.55 = f32[96,96]{1,0:T(8,128)S(1)} custom-call(f32[96,96]{1,0:T(8,128)S(1)} %fusion.18), custom_call_target="Cholesky" | custom-call | tf_op jit(solution)/shard_map/jit(cholesky)/cholesky | solution.py:144
  515.3 7.4 %custom-call.7 = f32[1,96,96]{1,2,0:T(8,128)S(1)} custom-call(f32[1,96,96]{2,1,0:T(8,128)S(1)} %get-tuple-element.21), custom_call_target="InvertDiagBlocksLowerTriangular" | custom-call | tf_op jit(solution)/shard_map/triangular_solve/custom-call.0 | solution.py:145
  (81 shorter events, 18.6 us)
Async XLA Ops:
  7.2 1.2 copy-start
  7.2 28.8 %reduce-scatter.5.cloned.1.call-start = ((), (), s32[]{:S(2)}) async-start(), calls=%async_computation.6 | async-start | bytes 786432 | tf_op jit(solution)/shard_map/reduce_scatter | solution.py:17
  10.6 86.1 %reduce-scatter.7.cloned.1.call-start = ((), (), s32[]{:S(2)}) async-start(), calls=%async_computation.7 | async-start | bytes 278528 | tf_op jit(solution)/shard_map/reduce_scatter | solution.py:17
  36.0 251.1 %reduce-scatter.9.cloned.1.call-start = ((), (), s32[]{:S(2)}) async-start(), calls=%async_computation.8 | async-start | bytes 786432 | tf_op jit(solution)/shard_map/reduce_scatter | solution.py:17
  178.7 0.7 copy-start.1
  273.3 74.3 %reduce-scatter.11.cloned.1.call-start = ((), (), s32[]{:S(2)}) async-start(), calls=%async_computation.9 | async-start | bytes 278528 | tf_op jit(solution)/shard_map/reduce_scatter | solution.py:17
Sparse Core Ops, SparseCore 0:
  10.8 25.1 reduce-scatter.4
  38.7 57.8 reduce-scatter.6
  273.4 13.5 reduce-scatter.8
  289.7 57.8 reduce-scatter.10
where the time goes:
time: 531 us; the launch traced here: 530 us
  blocking collectives  310 us (58%)
  waiting for transfers between devices  155 us (29%)
  other arithmetic  37 us (7%)
  between operations  14.1 us (3%)
  local copies, waits for them, and re-layouts  9.2 us (2%)
    reduce_scatter x4, waiting for transfers between devices, sum_in_order(): parts = lax.psum_scatter(parts, axes[k], scatter_dimension=0, tiled=True)  155 us
    psum x6, blocking collectives, by_axis(): shard = lax.psum(shard, axis)  149 us
    all_gather x6, blocking collectives, all_blocks(): parts = lax.all_gather(parts, axes[k])  111 us
    unnamed x2, blocking collectives  28.1 us
    all_to_all x2, blocking collectives, sent_to_all(): lax.all_to_all(jnp.broadcast_to(shard[None], (devices, *shard.shape)), ax...  21.9 us
    another operation x6, other arithmetic, local(): lower_factor = jnp.linalg.cholesky(gram_matrix)  18.9 us
    another operation x3, other arithmetic, local(): lax.linalg.triangular_solve(lower_factor, summed_back, left_side=True, lo...  15.4 us
  transfers between devices with their start and end apart: 4, of which 4 were waited for; matrix products, arithmetic and copies ran while one was open for 1% of the time, Pallas kernels for 0%

commit v1 on v0

--- a/solution.py
+++ b/solution.py
@@ -62,7 +62,7 @@
 
 def by_axis(shard, axes):
     for axis in axes:
-        shard = lax.psum(shard, axis)
+        shard = jnp.sum(lax.all_gather(shard, axis), axis=0)
     return shard
 
 

time: 531 us -> 479 us (0.902)
  blocking collectives: 310 us -> 257 us
    psum x6 -> x0, blocking collectives: 149 us -> none  [by_axis(): shard = lax.psum(shard, axis)]
    all_gather x0 -> x6, blocking collectives: none -> 95.4 us  [by_axis(): shard = jnp.sum(lax.all_gather(shard, axis), axis=0)]
where the time goes in v1:
time: 479 us; the launch traced here: 478 us
  blocking collectives  257 us (54%)
  waiting for transfers between devices  156 us (33%)
  other arithmetic  37.2 us (8%)
  between operations  14.1 us (3%)
  local copies, waits for them, and re-layouts  9.36 us (2%)
    reduce_scatter x4, waiting for transfers between devices, sum_in_order(): parts = lax.psum_scatter(parts, axes[k], scatter_dimension=0, tiled=True)  156 us
    all_gather x6, blocking collectives, all_blocks(): parts = lax.all_gather(parts, axes[k])  111 us
    all_gather x6, blocking collectives, by_axis(): shard = jnp.sum(lax.all_gather(shard, axis), axis=0)  95.4 us
    unnamed x2, blocking collectives  27.9 us
    all_to_all x2, blocking collectives, sent_to_all(): lax.all_to_all(jnp.broadcast_to(shard[None], (devices, *shard.shape)), ax...  22 us
    another operation x6, other arithmetic, local(): lower_factor = jnp.linalg.cholesky(gram_matrix)  18.9 us
    another operation x3, other arithmetic, local(): lax.linalg.triangular_solve(lower_factor, summed_back, left_side=True, lo...  15.4 us
  transfers between devices with their start and end apart: 4, of which 4 were waited for; matrix products, arithmetic and copies ran while one was open for 1% of the time, Pallas kernels for 0%

profile of v1, /device:TPU:1, one launch (start us, length us, event | category | flops | bytes accessed | tf_op | source)
XLA Modules:
  0.0 478.0 jit_solution(7793571975353201070)
XLA Ops:
  14.1 21.8 %reduce-scatter.5.cloned.1.call-done = f32[64,96,8]{1,2,0:T(8,128)} async-done(((f32[128,96,8]{1,2,0:T(8,128)}), f32[64,96,8]{1,2,0:T(8,128)}) %reduce-scatter.5.cloned.1.call-update) | async-done | bytes 196624 | tf_op jit(solution)/shard_map/reduce_scatter | solution.py:17
  37.7 59.0 %reduce-scatter.7.cloned.1.call-done = f32[4,96,8]{1,2,0:T(8,128)} async-done(((f32[64,96,8]{1,2,0:T(8,128)}), f32[4,96,8]{1,2,0:T(8,128)}) %reduce-scatter.7.cloned.1.call-update) | async-done | bytes 12304 | tf_op jit(solution)/shard_map/reduce_scatter | solution.py:17
  96.7 14.1 %all-reduce = f32[4,96,8]{1,2,0:T(8,128)S(1)} all-reduce(f32[4,96,8]{1,2,0:T(8,128)} %reduce-scatter.7.cloned.1.call-done), channel_id=14, replica_groups=mesh['row'=4,'col_0'=4,'col_1'=16,'col_2'=2] {'col_0'}, use_global_device_ids=true, to_apply=%region_2.3.clone | all-reduce | flops 3072 | bytes 24576
  111.5 8.4 %all_gather.68 = bf16[4,96,8]{1,2,0:T(8,128)(2,1)S(1)} all-gather(bf16[1,96,8]{1,2,0:T(8,128)(2,1)S(1)} %add_convert_fusion.1), channel_id=1, replica_groups=mesh['row'=4,'col_0'=4,'col_1'=16,'col_2'=2] {'col_0'}, dimensions={0}, use_global_device_ids=true | all-gather | bytes 7680 | tf_op jit(solution)/shard_map/all_gather | solution.py:41
  120.0 20.8 %all-gather = bf16[64,96,8]{1,2,0:T(8,128)(2,1)S(1)} all-gather(bf16[4,96,8]{1,2,0:T(8,128)(2,1)S(1)} %all_gather.68), channel_id=2, replica_groups=mesh['row'=4,'col_0'=4,'col_1'=16,'col_2'=2] {'col_1'}, dimensions={0}, use_global_device_ids=true | all-gather | bytes 104448 | tf_op jit(solution)/shard_map/all_gather | solution.py:41
  140.8 26.4 %all-gather.1 = bf16[32,4,96,8]{2,3,1,0:T(8,128)(2,1)S(1)} all-gather(bf16[16,4,96,8]{2,3,1,0:T(8,128)(2,1)S(1)} %bitcast.108), channel_id=3, replica_groups=mesh['row'=4,'col_0'=4,'col_1'=16,'col_2'=2] {'col_2'}, dimensions={0}, use_global_device_ids=true | all-gather | bytes 294912 | tf_op jit(solution)/shard_map/all_gather | solution.py:41
  167.7 11.0 %all_to_all.10 = bf16[4,96,512]{2,1,0:T(8,128)(2,1)S(1)} all-to-all(bf16[4,96,512]{2,1,0:T(8,128)(2,1)S(1)} %broadcast_in_dim.66), channel_id=1, replica_groups=mesh['row'=4,'col_0'=4,'col_1'=16,'col_2'=2] {'row'}, dimensions={0} | all-to-all | bytes 786432 | tf_op jit(solution)/shard_map/all_to_all | solution.py:54
  179.7 9.2 %all-gather.2 = f32[384,96]{1,0:T(8,128)S(1)} all-gather(f32[96,96]{1,0:T(8,128)S(1)} %fusion.8), channel_id=4, replica_groups=mesh['row'=4,'col_0'=4,'col_1'=16,'col_2'=2] {'col_0'}, dimensions={0}, use_global_device_ids=true | all-gather | bytes 184320 | tf_op jit(solution)/shard_map/all_gather | solution.py:65
  189.0 25.8 %all-gather.3 = f32[1536,96]{1,0:T(8,128)S(1)} all-gather(f32[96,96]{1,0:T(8,128)S(1)} %reduce_sum.93), channel_id=5, replica_groups=mesh['row'=4,'col_0'=4,'col_1'=16,'col_2'=2] {'col_1'}, dimensions={0}, use_global_device_ids=true | all-gather | bytes 626688 | tf_op jit(solution)/shard_map/all_gather | solution.py:65
  214.8 12.6 %all-gather.4 = f32[192,96]{1,0:T(8,128)S(1)} all-gather(f32[96,96]{1,0:T(8,128)S(1)} %reduce_sum.94), channel_id=6, replica_groups=mesh['row'=4,'col_0'=4,'col_1'=16,'col_2'=2] {'col_2'}, dimensions={0}, use_global_device_ids=true | all-gather | bytes 110592 | tf_op jit(solution)/shard_map/all_gather | solution.py:65
  227.6 8.8 %cholesky.44 = f32[96,96]{1,0:T(8,128)S(1)} custom-call(f32[96,96]{1,0:T(8,128)S(1)} %fusion.20), custom_call_target="Cholesky" | custom-call | tf_op jit(solution)/shard_map/jit(cholesky)/cholesky | solution.py:144
  237.7 7.4 %custom-call.6 = f32[1,96,96]{1,2,0:T(8,128)S(1)} custom-call(f32[1,96,96]{2,1,0:T(8,128)S(1)} %fusion.16), custom_call_target="InvertDiagBlocksLowerTriangular" | custom-call | tf_op jit(solution)/shard_map/triangular_solve/custom-call.0 | solution.py:145
  246.8 14.3 %reduce-scatter.9.cloned.1.call-done = f32[64,96,8]{1,2,0:T(8,128)} async-done(((f32[128,96,8]{1,2,0:T(8,128)}), f32[64,96,8]{1,2,0:T(8,128)}) %reduce-scatter.9.cloned.1.call-update) | async-done | bytes 196624 | tf_op jit(solution)/shard_map/reduce_scatter | solution.py:17
  261.2 60.8 %reduce-scatter.11.cloned.1.call-done = f32[4,96,8]{1,2,0:T(8,128)} async-done(((f32[64,96,8]{1,2,0:T(8,128)}), f32[4,96,8]{1,2,0:T(8,128)}) %reduce-scatter.11.cloned.1.call-update) | async-done | bytes 12304 | tf_op jit(solution)/shard_map/reduce_scatter | solution.py:17
  321.9 13.9 %all-reduce.1 = f32[4,96,8]{1,2,0:T(8,128)S(1)} all-reduce(f32[4,96,8]{1,2,0:T(8,128)} %reduce-scatter.11.cloned.1.call-done), channel_id=17, replica_groups=mesh['row'=4,'col_0'=4,'col_1'=16,'col_2'=2] {'col_0'}, use_global_device_ids=true, to_apply=%region_13.16.clone | all-reduce | flops 3072 | bytes 24576
  336.6 8.4 %all_gather.79 = bf16[4,96,8]{1,2,0:T(8,128)(2,1)S(1)} all-gather(bf16[1,96,8]{1,2,0:T(8,128)(2,1)S(1)} %add_convert_fusion), channel_id=1, replica_groups=mesh['row'=4,'col_0'=4,'col_1'=16,'col_2'=2] {'col_0'}, dimensions={0}, use_global_device_ids=true | all-gather | bytes 7680 | tf_op jit(solution)/shard_map/all_gather | solution.py:41
  345.0 20.9 %all-gather.5 = bf16[64,96,8]{1,2,0:T(8,128)(2,1)S(1)} all-gather(bf16[4,96,8]{1,2,0:T(8,128)(2,1)S(1)} %all_gather.79), channel_id=7, replica_groups=mesh['row'=4,'col_0'=4,'col_1'=16,'col_2'=2] {'col_1'}, dimensions={0}, use_global_device_ids=true | all-gather | bytes 104448 | tf_op jit(solution)/shard_map/all_gather | solution.py:41
  365.9 26.4 %all-gather.6 = bf16[32,4,96,8]{2,3,1,0:T(8,128)(2,1)S(1)} all-gather(bf16[16,4,96,8]{2,3,1,0:T(8,128)(2,1)S(1)} %bitcast.109), channel_id=8, replica_groups=mesh['row'=4,'col_0'=4,'col_1'=16,'col_2'=2] {'col_2'}, dimensions={0}, use_global_device_ids=true | all-gather | bytes 294912 | tf_op jit(solution)/shard_map/all_gather | solution.py:41
  392.7 11.0 %all_to_all.11 = bf16[4,96,512]{2,1,0:T(8,128)(2,1)S(1)} all-to-all(bf16[4,96,512]{2,1,0:T(8,128)(2,1)S(1)} %broadcast_in_dim.67), channel_id=1, replica_groups=mesh['row'=4,'col_0'=4,'col_1'=16,'col_2'=2] {'row'}, dimensions={0} | all-to-all | bytes 786432 | tf_op jit(solution)/shard_map/all_to_all | solution.py:54
  404.1 9.2 %all-gather.7 = f32[384,96]{1,0:T(8,128)S(1)} all-gather(f32[96,96]{1,0:T(8,128)S(1)} %fusion.5), channel_id=9, replica_groups=mesh['row'=4,'col_0'=4,'col_1'=16,'col_2'=2] {'col_0'}, dimensions={0}, use_global_device_ids=true | all-gather | bytes 184320 | tf_op jit(solution)/shard_map/all_gather | solution.py:65
  413.4 25.8 %all-gather.8 = f32[1536,96]{1,0:T(8,128)S(1)} all-gather(f32[96,96]{1,0:T(8,128)S(1)} %reduce_sum.97), channel_id=10, replica_groups=mesh['row'=4,'col_0'=4,'col_1'=16,'col_2'=2] {'col_1'}, dimensions={0}, use_global_device_ids=true | all-gather | bytes 626688 | tf_op jit(solution)/shard_map/all_gather | solution.py:65
  439.3 12.7 %all-gather.9 = f32[192,96]{1,0:T(8,128)S(1)} all-gather(f32[96,96]{1,0:T(8,128)S(1)} %reduce_sum.98), channel_id=11, replica_groups=mesh['row'=4,'col_0'=4,'col_1'=16,'col_2'=2] {'col_2'}, dimensions={0}, use_global_device_ids=true | all-gather | bytes 110592 | tf_op jit(solution)/shard_map/all_gather | solution.py:65
  452.2 8.8 %cholesky.55 = f32[96,96]{1,0:T(8,128)S(1)} custom-call(f32[96,96]{1,0:T(8,128)S(1)} %fusion.18), custom_call_target="Cholesky" | custom-call | tf_op jit(solution)/shard_map/jit(cholesky)/cholesky | solution.py:144
  463.0 7.4 %custom-call.7 = f32[1,96,96]{1,2,0:T(8,128)S(1)} custom-call(f32[1,96,96]{2,1,0:T(8,128)S(1)} %get-tuple-element.21), custom_call_target="InvertDiagBlocksLowerTriangular" | custom-call | tf_op jit(solution)/shard_map/triangular_solve/custom-call.0 | solution.py:145
  (89 shorter events, 19.0 us)
Async XLA Ops:
  7.2 1.2 copy-start
  7.2 28.8 %reduce-scatter.5.cloned.1.call-start = ((), (), s32[]{:S(2)}) async-start(), calls=%async_computation.6 | async-start | bytes 786432 | tf_op jit(solution)/shard_map/reduce_scatter | solution.py:17
  10.6 86.1 %reduce-scatter.7.cloned.1.call-start = ((), (), s32[]{:S(2)}) async-start(), calls=%async_computation.7 | async-start | bytes 278528 | tf_op jit(solution)/shard_map/reduce_scatter | solution.py:17
  36.0 225.2 %reduce-scatter.9.cloned.1.call-start = ((), (), s32[]{:S(2)}) async-start(), calls=%async_computation.8 | async-start | bytes 786432 | tf_op jit(solution)/shard_map/reduce_scatter | solution.py:17
  178.7 0.7 copy-start.1
  246.8 75.2 %reduce-scatter.11.cloned.1.call-start = ((), (), s32[]{:S(2)}) async-start(), calls=%async_computation.9 | async-start | bytes 278528 | tf_op jit(solution)/shard_map/reduce_scatter | solution.py:17
Sparse Core Ops, SparseCore 0:
  10.8 25.1 reduce-scatter.4
  38.7 57.8 reduce-scatter.6
  246.9 14.1 reduce-scatter.8
  263.8 58.1 reduce-scatter.10
